TPU v7x, 512 devices: a whole 4x8x8 slice. The times are simulated.
512 devices in a mesh: seq: 64 (over y, z), mp: 8 (over x, core).
Axes of the slice: x: 4, y: 8, z: 8, core: 2. Of those that a mesh axis runs over, the one named last changes fastest.
Arguments:
- patch_states: bfloat16 [32768, 2048], P('seq'), may hold values from -6 to 6
- mlp_gain: bfloat16 [2048], replicated, may hold values from 0.099609375 to 1.8984375
- up_weight: bfloat16 [2048, 7168], P('seq', 'mp')
- down_weight: bfloat16 [7168, 2048], P('mp', 'seq')
- kv_gain: bfloat16 [2048], replicated, may hold values from 0.099609375 to 1.8984375
- kv_weight: bfloat16 [2048, 2048], P(None, 'mp'), may hold values from -0.125 to 0.125
- byte_states: bfloat16 [65536, 1024], P('seq'), may hold values from -6 to 6
- query_weight: bfloat16 [1024, 1024], P(None, 'mp'), may hold values from -0.1875 to 0.1875
- out_weight: bfloat16 [1024, 1024], P('mp'), may hold values from -0.75 to 0.75
- patch_counts: int32 [64], P('seq'), may hold values from 256 to 512, as said below
- byte_patch: int32 [65536], P('seq'), may hold values from 0 to 511, as said below
Outputs:
- decoded: bfloat16 [65536, 1024], P(('seq', 'mp'))
Inputs may be any that keep to these rules, and one draw needn't show every extreme that they name: `patch_counts`: exactly 512 in some block and exactly 256 in another, in every draw. `byte_patch`: within each seq block of 1024 bytes the values start at 0, never fall, rise by at most one from one byte to the next, and end at that block's patch count minus one.
All inputs are finite; a program needn't handle non-finite values.
Results may differ from a plain program's by a relative error of at most 0.02.
Values may be sent and summed in bfloat16 or wider, within the bound.
No kernel may reach another device: no remote copies, remote signals or barrier semaphores. Data moves between devices by JAX's collectives and lax.ppermute only.
A program may use at most 64 MiB of HBM per device.

v0:
```python
import math
import jax
import jax.numpy as jnp
from jax import lax
from jax.sharding import PartitionSpec as P

HS = 128
WIN = 1024


def entering(value, axis, join, neutral):
    count, mine = (lax.axis_size(axis), lax.axis_index(axis))
    pieces = jax.tree.map(lambda part: lax.all_gather(part, axis), value)
    so_far = jax.tree.map(
        lambda part, zero: jnp.full_like(part, 0) + jnp.asarray(zero, part.dtype), value, neutral
    )

    def step(position, so_far):
        longer = join(so_far, jax.tree.map(lambda part: part[position], pieces))
        return jax.tree.map(lambda new, old: jnp.where(position < mine, new, old), longer, so_far)

    return lax.fori_loop(0, count - 1, step, so_far)


def from_behind(value, axis, steps):
    count = lax.axis_size(axis)
    leading, last = (max(0, -steps), min(count, count - steps))
    return lax.ppermute(value, axis, [(source, source + steps) for source in range(leading, last)])


def scale_rows(values, gain):
    return values * lax.rsqrt(jnp.mean(values * values, axis=-1, keepdims=True) + 1e-05) * gain


def unit_rows(values):
    return values * lax.rsqrt(jnp.mean(values * values, axis=-1, keepdims=True) + 1e-06)


def on_device(
    patch_states,
    mlp_gain,
    up_weight,
    down_weight,
    kv_gain,
    kv_weight,
    byte_states,
    query_weight,
    out_weight,
    patch_counts,
    byte_patch,
):
    patch_rows = patch_states.shape[0]
    normed = scale_rows(patch_states.astype(jnp.float32), mlp_gain.astype(jnp.float32)).astype(
        jnp.bfloat16
    )
    preact = jnp.dot(
        normed,
        lax.all_gather(up_weight, "seq", axis=0, tiled=True),
        preferred_element_type=jnp.float32,
    )
    hidden = jax.nn.gelu(preact, approximate=False).astype(jnp.bfloat16)
    kv_scale = kv_gain.astype(jnp.float32)
    partial_value = jnp.dot(
        hidden,
        lax.all_gather(down_weight, "seq", axis=1, tiled=True),
        preferred_element_type=jnp.float32,
    )
    mixed_out = lax.psum(partial_value.astype(jnp.bfloat16), "mp").astype(jnp.float32)
    kv_in = scale_rows(patch_states.astype(jnp.float32) + mixed_out, kv_scale).astype(jnp.bfloat16)
    heads_here = kv_weight.shape[1] // (2 * HS)
    projected = jnp.dot(kv_in, kv_weight, preferred_element_type=jnp.float32).reshape(
        patch_rows, heads_here, 2, HS
    )
    keys = unit_rows(projected[:, :, 0])
    kv_pack = (
        jnp.stack([keys, projected[:, :, 1]], axis=2)
        .astype(jnp.bfloat16)
        .reshape(patch_rows, heads_here * 2 * HS)
    )
    bytes_here = byte_states.shape[0]
    query_proj = jnp.dot(byte_states, query_weight, preferred_element_type=jnp.float32).reshape(
        bytes_here, heads_here, HS
    )
    queries = unit_rows(query_proj).astype(jnp.bfloat16)
    depth_back = (WIN + patch_rows // 2 - 2) // (patch_rows // 2)
    own_count = patch_counts[0]
    slots = jnp.arange(depth_back, dtype=jnp.int32)

    def join_windows(earlier_part, later_part):
        early_vals, early_len = earlier_part
        late_vals, late_len = later_part
        from_late = slots >= depth_back - late_len
        wanted = slots + late_len
        early_pick = jnp.sum(
            jnp.where(slots[None, :] == wanted[:, None], early_vals[None, :], 0), axis=1
        ).astype(jnp.int32)
        joined = jnp.where(from_late, late_vals, early_pick).astype(jnp.int32)
        return (joined, jnp.minimum(early_len + late_len, depth_back).astype(jnp.int32))

    own_window = jnp.where(slots == depth_back - 1, own_count, 0)
    empty_window = (jnp.zeros((depth_back,), jnp.int32), jnp.zeros((), jnp.int32))
    prior_counts, prior_len = entering(
        (own_window, jnp.ones((), jnp.int32)), "seq", join_windows, empty_window
    )
    earlier = []
    forwarded = kv_pack
    for offset_back in range(1, depth_back + 1):
        forwarded = from_behind(forwarded, "seq", 1)
        earlier.append(forwarded)
    score_scale = 2.0 / math.sqrt(HS)
    positions = jnp.arange(patch_rows, dtype=jnp.int32)
    numerator = jnp.zeros((bytes_here, heads_here, HS), jnp.float32)
    denominator = jnp.zeros((heads_here, bytes_here), jnp.float32)
    for distance, kv_block in enumerate([kv_pack] + earlier):
        if distance == 0:
            first_id = jnp.zeros((), jnp.int32)
            live_count = own_count
        else:
            first_id = -jnp.sum(prior_counts[depth_back - distance :]).astype(jnp.int32)
            live_count = prior_counts[depth_back - distance]
        key_ids = first_id + positions
        usable = (
            (positions < live_count)[None, :]
            & (key_ids[None, :] <= byte_patch[:, None])
            & (key_ids[None, :] > byte_patch[:, None] - WIN)
        )
        kv_parts = kv_block.reshape(patch_rows, heads_here, 2, HS)
        scores = (
            jnp.einsum(
                "bhd,phd->hbp", queries, kv_parts[:, :, 0], preferred_element_type=jnp.float32
            )
            * score_scale
        )
        weights = jnp.where(usable[None], jnp.exp(scores), 0.0)
        numerator = numerator + jnp.einsum(
            "hbp,phd->bhd",
            weights.astype(jnp.bfloat16),
            kv_parts[:, :, 1],
            preferred_element_type=jnp.float32,
        )
        denominator = denominator + jnp.sum(weights, axis=-1)
    attended = (
        (numerator / jnp.transpose(denominator)[:, :, None])
        .astype(jnp.bfloat16)
        .reshape(bytes_here, heads_here * HS)
    )
    decoded = lax.psum_scatter(
        jnp.dot(attended, out_weight, preferred_element_type=jnp.float32).astype(jnp.bfloat16),
        "mp",
        scatter_dimension=0,
        tiled=True,
    )
    return decoded


def solution(mesh):
    in_specs = (
        P("seq", None),
        P(),
        P("seq", "mp"),
        P("mp", "seq"),
        P(),
        P(None, "mp"),
        P("seq", None),
        P(None, "mp"),
        P("mp", None),
        P("seq"),
        P("seq"),
    )
    out_specs = P(("seq", "mp"), None)
    return jax.shard_map(
        on_device, mesh=mesh, in_specs=in_specs, out_specs=out_specs, check_vma=False
    )
```

profile of v0, /device:TPU:8, one launch (start us, length us, event | category | flops | bytes accessed | tf_op | source)
XLA Modules:
  0.0 416.1 jit_solution(15715362171986909808)
XLA Ops:
  6.5 0.7 all-gather.4.cloned.1.call-update
  7.3 0.7 all-gather.6.cloned.1.call-update
  8.7 48.6 %all-gather = s32[64,1,4]{2,1,0:T(1,128)S(1)} all-gather(s32[1,1,4]{2,1,0:T(1,128)S(1)} %fusion.71), channel_id=1, replica_groups=mesh['seq'=64,'mp'=8] {'seq'}, dimensions={0}, use_global_device_ids=true | all-gather | bytes 1040 | tf_op jit(solution)/shard_map/all_gather | solution.py:13
  57.3 1.3 dynamic-slice
  58.7 0.8 dynamic-update-slice
  59.5 23.7 %all-reduce = s32[64]{0:T(128)S(1)} all-reduce(s32[64]{0:T(128)S(1)} %dynamic-update-slice), channel_id=1, replica_groups=mesh['seq'=64,'mp'=8] {'seq'}, use_global_device_ids=true, to_apply=%add | all-reduce | flops 64 | bytes 512
  83.2 130.9 %while.15 = (s32[]{:T(128)}, s32[4]{0:T(128)S(1)}, s32[]{:T(128)}, s32[64]{0:T(128)S(1)}, s32[64,4]{1,0:T(8,128)S(1)}, /*index=5*/s32[]{:T(128)}, s32[]{:T(128)}, s32[]{:T(128)}) while((s32[]{:T(128)}, s32[4]{0:T(128)S(1)}, s32[]{:T(128)}, s32[64]{0:T(128)S(1)}, s32[64,4]{1,0:T(8,128)S(1)}, /*index=5*/s32[]{:T(128)}, ...), condition=%wide.region_7.8_spmd.clone.clone, body=%wide.region_5.7_spmd.clone.clone.sunk | while | flops 69 | bytes 301 | solution.py:22
  85.3 0.6 dynamic_slice.22
  87.4 0.6 dynamic_slice.22
  91.5 0.6 dynamic_slice.22
  95.7 0.6 dynamic_slice.22
  97.8 0.6 dynamic_slice.22
  101.9 0.6 dynamic_slice.22
  106.1 0.6 dynamic_slice.22
  108.1 0.6 dynamic_slice.22
  110.2 0.6 dynamic_slice.22
  112.3 0.6 dynamic_slice.22
  116.5 0.6 dynamic_slice.22
  120.6 0.6 dynamic_slice.22
  122.7 0.6 dynamic_slice.22
  124.8 0.6 dynamic_slice.22
  126.8 0.6 dynamic_slice.22
  128.9 0.6 dynamic_slice.22
  133.1 0.6 dynamic_slice.22
  137.2 0.6 dynamic_slice.22
  139.3 0.6 dynamic_slice.22
  143.5 0.6 dynamic_slice.22
  147.6 0.6 dynamic_slice.22
  149.7 0.6 dynamic_slice.22
  151.8 0.6 dynamic_slice.22
  153.9 0.6 dynamic_slice.22
  155.9 0.6 dynamic_slice.22
  158.0 0.6 dynamic_slice.22
  162.2 0.6 dynamic_slice.22
  214.1 0.7 convert_element_type.71
  214.8 0.7 convert_element_type.76
  215.5 0.7 reduce_sum.131
  216.2 0.7 fusion.102
  218.1 0.8 slice_reduce_fusion
  219.6 0.8 slice_reduce_fusion.1
  221.0 0.7 iota_compare_fusion.6
  221.7 0.7 iota_compare_fusion.3
  223.6 2.1 fusion.2
  225.8 13.4 %convolution_convert_fusion = bf16[512,2048]{1,0:T(8,128)(2,1)} fusion(bf16[896,2048]{0,1:T(8,128)(2,1)} %all-gather.6.cloned.1.call-done, bf16[2048,896]{1,0:T(8,128)(2,1)} %all-gather.4.cloned.1.call-done, bf16[512,2048]{1,0:T(8,128)(2,1)} %param.13, f32[2048]{0:T(1024)S(1)} %convert_element_type.71, f32[512]{0:T(512)S(1)} %add_rsqrt_fusion.3), kind=kOutput, calls=%fused_computation.15 | convolution fusion | flops 3793158144 | bytes 11544576 | tf_op jit(solution)/shard_map/dot_general | solution.py:63
  239.3 0.8 copy-done.4
  240.1 0.8 multiply_reduce_fusion.1
  241.1 70.2 %all-reduce.3.cloned.1.call-done = bf16[512,2048]{1,0:T(8,128)(2,1)} async-done(((bf16[512,2048]{1,0:T(8,128)(2,1)}), bf16[512,2048]{1,0:T(8,128)(2,1)}) %all-reduce.3.cloned.1.call-update) | async-done | bytes 2097168 | tf_op jit(solution)/shard_map/psum | solution.py:68
  311.2 3.1 multiply_reduce_fusion
  314.7 1.2 fusion.5
  316.0 3.7 collective-permute-start
  319.7 1.1 fusion.106
  321.2 5.2 %collective-permute-done = bf16[512,256]{0,1:T(8,128)(2,1)S(1)} collective-permute-done((bf16[512,256]{0,1:T(8,128)(2,1)S(1)}, bf16[512,256]{0,1:T(8,128)(2,1)S(1)}, u32[]{:S(2)}, u32[]{:S(2)}) %collective-permute-start) | collective-permute-done | bytes 262176 | tf_op jit(solution)/shard_map/ppermute | solution.py:28
  326.4 1.0 fusion.107
  327.4 1.9 collective-permute-start.1
  329.7 8.1 %collective-permute-done.1 = bf16[512,256]{0,1:T(8,128)(2,1)S(1)} collective-permute-done((bf16[512,256]{0,1:T(8,128)(2,1)S(1)}, bf16[512,256]{0,1:T(8,128)(2,1)S(1)}, u32[]{:S(2)}, u32[]{:S(2)}) %collective-permute-start.1) | collective-permute-done | bytes 262176 | tf_op jit(solution)/shard_map/ppermute | solution.py:28
  337.8 1.0 fusion.105
  338.8 1.9 collective-permute-start.2
  341.1 8.1 %collective-permute-done.2 = bf16[512,256]{0,1:T(8,128)(2,1)S(1)} collective-permute-done((bf16[512,256]{0,1:T(8,128)(2,1)S(1)}, bf16[512,256]{0,1:T(8,128)(2,1)S(1)}, u32[]{:S(2)}, u32[]{:S(2)}) %collective-permute-start.2) | collective-permute-done | bytes 262176 | tf_op jit(solution)/shard_map/ppermute | solution.py:28
  349.2 1.0 fusion.104
  350.3 1.9 collective-permute-start.3
  352.5 8.1 %collective-permute-done.3 = bf16[512,256]{0,1:T(8,128)(2,1)S(1)} collective-permute-done((bf16[512,256]{0,1:T(8,128)(2,1)S(1)}, bf16[512,256]{0,1:T(8,128)(2,1)S(1)}, u32[]{:S(2)}, u32[]{:S(2)}) %collective-permute-start.3) | collective-permute-done | bytes 262176 | tf_op jit(solution)/shard_map/ppermute | solution.py:28
  360.7 2.0 fusion.103
  362.7 3.5 convolution_convert_fusion.1
  366.3 43.3 %reduce-scatter.2.cloned.1.call-done = bf16[128,1024]{1,0:T(8,128)(2,1)} async-done(((bf16[1024,1024]{1,0:T(8,128)(2,1)}), bf16[128,1024]{1,0:T(8,128)(2,1)}) %reduce-scatter.2.cloned.1.call-update) | async-done | bytes 262160 | tf_op jit(solution)/shard_map/reduce_scatter | solution.py:147
  (270 shorter events, 76.2 us)
Async XLA Ops:
  6.5 232.7 %copy-start = (bf16[1024,1024]{1,0:T(8,128)(2,1)S(1)}, bf16[1024,1024]{1,0:T(8,128)(2,1)}, u32[]{:S(2)}) copy-start(bf16[1024,1024]{1,0:T(8,128)(2,1)} %param.19) | copy-start | bytes 6291460
  6.5 219.2 %all-gather.4.cloned.1.call-start = ((), (), s32[]{:S(2)}) async-start(), calls=%async_computation.1 | async-start | bytes 3727360 | tf_op jit(solution)/shard_map/all_gather | solution.py:58
  7.3 218.5 %all-gather.6.cloned.1.call-start = ((), (), s32[]{:S(2)}) async-start(), calls=%async_computation.2 | async-start | bytes 3727360 | tf_op jit(solution)/shard_map/all_gather | solution.py:65
  8.0 303.2 %all-reduce.3.cloned.1.call-start = ((), (), s32[]{:S(2)}) async-start(), calls=%async_computation.3 | async-start | bytes 4194304 | tf_op jit(solution)/shard_map/psum | solution.py:68
  239.2 0.9 copy-start.4
  239.2 1.8 copy-start.5
  239.2 170.4 %reduce-scatter.2.cloned.1.call-start = ((), (), s32[]{:S(2)}) async-start(), calls=%async_computation.4 | async-start | bytes 2359296 | tf_op jit(solution)/shard_map/reduce_scatter | solution.py:147
  240.1 74.2 %copy-start.6 = (bf16[2048,256]{1,0:T(8,128)(2,1)S(1)}, bf16[2048,256]{1,0:T(8,128)(2,1)}, u32[]{:S(2)}) copy-start(bf16[2048,256]{1,0:T(8,128)(2,1)} %param.18) | copy-start | bytes 3145732
  311.2 3.1 copy-start.1
  311.2 3.5 copy-start.2
  316.0 10.4 %collective-permute-start = (bf16[512,256]{0,1:T(8,128)(2,1)S(1)}, bf16[512,256]{0,1:T(8,128)(2,1)S(1)}, u32[]{:S(2)}, u32[]{:S(2)}) collective-permute-start(bf16[512,256]{0,1:T(8,128)(2,1)S(1)} %bitcast.99), channel_id=1, source_target_pairs={{0,8},{8,16},{16,24},{24,32},{32,40},{40,48},{48,56},{56,64},{64,7... | collective-permute-start | bytes 786440 | tf_op jit(solution)/shard_map/ppermute | solution.py:28
  327.4 10.4 %collective-permute-start.1 = (bf16[512,256]{0,1:T(8,128)(2,1)S(1)}, bf16[512,256]{0,1:T(8,128)(2,1)S(1)}, u32[]{:S(2)}, u32[]{:S(2)}) collective-permute-start(bf16[512,256]{0,1:T(8,128)(2,1)S(1)} %collective-permute-done), channel_id=1, source_target_pairs={{0,8},{8,16},{16,24},{24,32},{32,40},{40,48},{48,56},{56,64},{64,7... | collective-permute-start | bytes 786440 | tf_op jit(solution)/shard_map/ppermute | solution.py:28
  338.8 10.4 %collective-permute-start.2 = (bf16[512,256]{0,1:T(8,128)(2,1)S(1)}, bf16[512,256]{0,1:T(8,128)(2,1)S(1)}, u32[]{:S(2)}, u32[]{:S(2)}) collective-permute-start(bf16[512,256]{0,1:T(8,128)(2,1)S(1)} %collective-permute-done.1), channel_id=1, source_target_pairs={{0,8},{8,16},{16,24},{24,32},{32,40},{40,48},{48,56},{56,64},{64,7... | collective-permute-start | bytes 786440 | tf_op jit(solution)/shard_map/ppermute | solution.py:28
  350.3 10.4 %collective-permute-start.3 = (bf16[512,256]{0,1:T(8,128)(2,1)S(1)}, bf16[512,256]{0,1:T(8,128)(2,1)S(1)}, u32[]{:S(2)}, u32[]{:S(2)}) collective-permute-start(bf16[512,256]{0,1:T(8,128)(2,1)S(1)} %collective-permute-done.2), channel_id=1, source_target_pairs={{0,8},{8,16},{16,24},{24,32},{32,40},{40,48},{48,56},{56,64},{64,7... | collective-permute-start | bytes 786440 | tf_op jit(solution)/shard_map/ppermute | solution.py:28
  360.7 2.0 copy-start.3
Sparse Core Ops, SparseCore 0:
  10.4 90.1 all-gather.3
  103.6 82.9 all-gather.5
  239.3 71.8 all-reduce.2
  366.4 43.1 reduce-scatter.1
where the time goes:
time: 418 us; the launch traced here: 416 us
  waiting for transfers between devices  145 us (35%)
  blocking collectives  72.3 us (17%)
  other arithmetic  62.3 us (15%)
  local copies, waits for them, and re-layouts  43 us (10%)
  loops' own time  41.1 us (10%)
  matrix products  26.5 us (6%)
  between operations  16.7 us (4%)
  starting transfers between devices  9.62 us (2%)
    psum x1, waiting for transfers between devices, on_device(): lax.psum(partial_value.astype(jnp.bfloat16), 'mp').astype(jnp.float32)  70.2 us
    all_gather x1, blocking collectives, entering(): pieces = jax.tree.map(lambda part: lax.all_gather(part, axis), value)  48.6 us
    reduce_scatter x1, waiting for transfers between devices, on_device(): lax.psum_scatter(jnp.dot(attended, out_weight, preferred_element_type=jnp...  43.3 us
    another operation x1, loops' own time, entering(): return lax.fori_loop(0, count - 1, step, so_far)  41.1 us
    dynamic_slice x63, local copies, waits for them, and re-layouts, step(): longer = join(so_far, jax.tree.map(lambda part: part[position], pieces))  39 us
    while x63, other arithmetic  38.5 us
    ppermute x4, waiting for transfers between devices, from_behind(): lax.ppermute(value, axis, [(source, source + steps) for source in range(l...  29.6 us
    unnamed x1, blocking collectives  23.7 us
  transfers between devices with their start and end apart: 8, of which 6 were waited for; matrix products, arithmetic and copies ran while one was open for 25% of the time, Pallas kernels for 0%

commit v1 on v0

--- a/solution.py
+++ b/solution.py
@@ -6,6 +6,11 @@
 
 HS = 128
 WIN = 1024
+
+
+def summed_here(x, axis):
+    shards = lax.all_gather(x, axis)
+    return jnp.sum(shards, axis=0)
 
 
 def entering(value, axis, join, neutral):
@@ -65,7 +70,7 @@
         lax.all_gather(down_weight, "seq", axis=1, tiled=True),
         preferred_element_type=jnp.float32,
     )
-    mixed_out = lax.psum(partial_value.astype(jnp.bfloat16), "mp").astype(jnp.float32)
+    mixed_out = summed_here(partial_value.astype(jnp.bfloat16), "mp").astype(jnp.float32)
     kv_in = scale_rows(patch_states.astype(jnp.float32) + mixed_out, kv_scale).astype(jnp.bfloat16)
     heads_here = kv_weight.shape[1] // (2 * HS)
     projected = jnp.dot(kv_in, kv_weight, preferred_element_type=jnp.float32).reshape(

time: 418 us -> 444 us (1.062)
  waiting for transfers between devices: 145 us -> 170 us
  other arithmetic: 62.3 us -> 69 us
  local copies, waits for them, and re-layouts: 43 us -> 38.3 us
    all_gather x1, waiting for transfers between devices: 0.02 us -> 85.8 us  [on_device(): lax.all_gather(down_weight, 'seq', axis=1, tiled=True)]
    psum x1 -> x0, waiting for transfers between devices: 70.2 us -> none  [on_device(): lax.psum(partial_value.astype(jnp.bfloat16), 'mp').astype(jnp.float32)]
    all_gather x1, waiting for transfers between devices: 0.02 us -> 13.5 us  [on_device(): lax.all_gather(up_weight, 'seq', axis=0, tiled=True)]
    reduce_sum x0 -> x1, other arithmetic: none -> 10.8 us  [summed_here(): return jnp.sum(shards, axis=0)]
    unnamed x1, blocking collectives: 23.7 us -> 30.7 us
    all_gather x1, blocking collectives: 48.6 us -> 42 us  [entering(): pieces = jax.tree.map(lambda part: lax.all_gather(part, axis), value)]
    reduce_scatter x1, waiting for transfers between devices: 43.3 us -> 38.7 us  [on_device(): lax.psum_scatter(jnp.dot(attended, out_weight, preferred_element_type=jnp...]
  transfers between devices with their start and end apart: 8 -> 8, of which waited for: 6 -> 7; matrix products, arithmetic and copies ran while one was open for 25% -> 22% of each run, Pallas kernels for 0% -> 0%
where the time goes in v1:
time: 444 us; the launch traced here: 441 us
  waiting for transfers between devices  170 us (38%)
  blocking collectives  72.7 us (16%)
  other arithmetic  69 us (16%)
  local copies, waits for them, and re-layouts  38.3 us (9%)
  loops' own time  37.3 us (8%)
  matrix products  27.7 us (6%)
  between operations  16.6 us (4%)
  starting transfers between devices  8.67 us (2%)
    all_gather x1, waiting for transfers between devices, on_device(): lax.all_gather(down_weight, 'seq', axis=1, tiled=True)  85.8 us
    all_gather x1, blocking collectives, entering(): pieces = jax.tree.map(lambda part: lax.all_gather(part, axis), value)  42 us
    reduce_scatter x1, waiting for transfers between devices, on_device(): lax.psum_scatter(jnp.dot(attended, out_weight, preferred_element_type=jnp...  38.7 us
    another operation x1, loops' own time, entering(): return lax.fori_loop(0, count - 1, step, so_far)  37.3 us
    dynamic_slice x63, local copies, waits for them, and re-layouts, step(): longer = join(so_far, jax.tree.map(lambda part: part[position], pieces))  35.2 us
    while x63, other arithmetic  34.7 us
    ppermute x4, waiting for transfers between devices, from_behind(): lax.ppermute(value, axis, [(source, source + steps) for source in range(l...  30.9 us
    unnamed x1, blocking collectives  30.7 us
  transfers between devices with their start and end apart: 8, of which 7 were waited for; matrix products, arithmetic and copies ran while one was open for 22% of the time, Pallas kernels for 0%

profile of v1, /device:TPU:8, one launch (start us, length us, event | category | flops | bytes accessed | tf_op | source)
XLA Modules:
  0.0 440.6 jit_solution(13266938854479148277)
XLA Ops:
  6.5 0.7 all-gather.6.cloned.1.call-update
  7.3 0.7 all-gather.8.cloned.1.call-update
  8.1 0.7 convert_element_type.73
  8.8 0.7 convert_element_type.78
  10.1 1.3 dynamic-slice
  11.5 0.8 dynamic-update-slice
  12.3 30.7 %all-reduce = s32[64]{0:T(128)S(1)} all-reduce(s32[64]{0:T(128)S(1)} %dynamic-update-slice), channel_id=1, replica_groups=mesh['seq'=64,'mp'=8] {'seq'}, use_global_device_ids=true, to_apply=%add | all-reduce | flops 64 | bytes 512
  43.0 42.0 %all-gather.1 = s32[64,1,4]{2,1,0:T(1,128)S(1)} all-gather(s32[1,1,4]{2,1,0:T(1,128)S(1)} %fusion.71), channel_id=1, replica_groups=mesh['seq'=64,'mp'=8] {'seq'}, dimensions={0}, use_global_device_ids=true | all-gather | bytes 1040 | tf_op jit(solution)/shard_map/all_gather | solution.py:18
  85.0 2.1 fusion.2
  87.1 13.5 %all-gather.6.cloned.1.call-done = bf16[2048,896]{1,0:T(8,128)(2,1)} async-done(((bf16[32,896]{1,0:T(8,128)(2,1)}), bf16[2048,896]{1,0:T(8,128)(2,1)}) %all-gather.6.cloned.1.call-update) | async-done | bytes 3670032 | tf_op jit(solution)/shard_map/all_gather | solution.py:63
  100.6 85.8 %all-gather.8.cloned.1.call-done = bf16[896,2048]{0,1:T(8,128)(2,1)} async-done(((bf16[896,32]{0,1:T(8,128)(2,1)}), bf16[896,2048]{0,1:T(8,128)(2,1)}) %all-gather.8.cloned.1.call-update) | async-done | bytes 3670032 | tf_op jit(solution)/shard_map/all_gather | solution.py:70
  186.4 13.4 %convolution_convert_fusion = bf16[512,2048]{1,0:T(8,128)(2,1)} fusion(bf16[896,2048]{0,1:T(8,128)(2,1)} %all-gather.8.cloned.1.call-done, bf16[2048,896]{1,0:T(8,128)(2,1)} %all-gather.6.cloned.1.call-done, bf16[512,2048]{1,0:T(8,128)(2,1)} %param.13, f32[2048]{0:T(1024)S(1)} %convert_element_type.73, f32[512]{0:T(512)S(1)} %add_rsqrt_fusion.3), kind=kOutput, calls=%fused_computation.15 | convolution fusion | flops 3793158144 | bytes 11544576 | tf_op jit(solution)/shard_map/dot_general | solution.py:68
  200.0 119.4 %while.15 = (s32[]{:T(128)}, s32[4]{0:T(128)S(1)}, s32[]{:T(128)}, s32[64]{0:T(128)S(1)}, s32[64,4]{1,0:T(8,128)S(1)}, /*index=5*/s32[]{:T(128)}, s32[]{:T(128)}, s32[]{:T(128)}) while((s32[]{:T(128)}, s32[4]{0:T(128)S(1)}, s32[]{:T(128)}, s32[64]{0:T(128)S(1)}, s32[64,4]{1,0:T(8,128)S(1)}, /*index=5*/s32[]{:T(128)}, ...), condition=%wide.region_7.8_spmd.clone.clone, body=%wide.region_5.7_spmd.clone.clone.sunk | while | flops 69 | bytes 301 | solution.py:27
  200.0 0.6 dynamic_slice.22
  201.9 0.6 dynamic_slice.22
  203.8 0.6 dynamic_slice.22
  205.7 0.6 dynamic_slice.22
  207.6 0.6 dynamic_slice.22
  209.5 0.6 dynamic_slice.22
  211.4 0.6 dynamic_slice.22
  213.3 0.6 dynamic_slice.22
  215.2 0.6 dynamic_slice.22
  217.1 0.6 dynamic_slice.22
  219.0 0.6 dynamic_slice.22
  220.9 0.6 dynamic_slice.22
  222.8 0.6 dynamic_slice.22
  224.7 0.6 dynamic_slice.22
  226.6 0.6 dynamic_slice.22
  228.5 0.6 dynamic_slice.22
  230.4 0.6 dynamic_slice.22
  232.3 0.6 dynamic_slice.22
  234.2 0.6 dynamic_slice.22
  236.1 0.6 dynamic_slice.22
  238.0 0.6 dynamic_slice.22
  239.8 0.6 dynamic_slice.22
  258.8 0.6 dynamic_slice.22
  275.8 0.6 dynamic_slice.22
  300.5 0.6 dynamic_slice.22
  319.4 0.6 reduce_sum.144
  320.1 0.6 fusion.102
  321.9 0.7 slice_reduce_fusion
  323.3 0.7 slice_reduce_fusion.1
  324.6 0.6 iota_compare_fusion.6
  325.2 0.6 iota_compare_fusion.3
  325.8 0.6 iota_compare_fusion.4
  327.1 0.8 multiply_reduce_fusion.1
  328.1 10.8 %reduce_sum.138 = bf16[512,2048]{1,0:T(8,128)(2,1)} reduce(bf16[8,512,2048]{2,1,0:T(8,128)(2,1)} %bitcast.98, bf16[]{:T(256)} %constant.113.clone.1), dimensions={0}, to_apply=%region_1.0 | reduce | flops 7340032 | bytes 18874370 | tf_op jit(solution)/shard_map/reduce_sum | solution.py:13
  338.9 3.1 multiply_reduce_fusion
  342.4 2.4 fusion.5
  344.9 2.6 collective-permute-start
  347.5 1.1 fusion.106
  348.9 6.3 %collective-permute-done = bf16[512,256]{0,1:T(8,128)(2,1)S(1)} collective-permute-done((bf16[512,256]{0,1:T(8,128)(2,1)S(1)}, bf16[512,256]{0,1:T(8,128)(2,1)S(1)}, u32[]{:S(2)}, u32[]{:S(2)}) %collective-permute-start) | collective-permute-done | bytes 262176 | tf_op jit(solution)/shard_map/ppermute | solution.py:33
  355.3 1.0 fusion.107
  356.3 1.9 collective-permute-start.1
  358.6 8.1 %collective-permute-done.1 = bf16[512,256]{0,1:T(8,128)(2,1)S(1)} collective-permute-done((bf16[512,256]{0,1:T(8,128)(2,1)S(1)}, bf16[512,256]{0,1:T(8,128)(2,1)S(1)}, u32[]{:S(2)}, u32[]{:S(2)}) %collective-permute-start.1) | collective-permute-done | bytes 262176 | tf_op jit(solution)/shard_map/ppermute | solution.py:33
  366.7 1.0 fusion.105
  367.7 1.9 collective-permute-start.2
  370.0 8.3 %collective-permute-done.2 = bf16[512,256]{0,1:T(8,128)(2,1)S(1)} collective-permute-done((bf16[512,256]{0,1:T(8,128)(2,1)S(1)}, bf16[512,256]{0,1:T(8,128)(2,1)S(1)}, u32[]{:S(2)}, u32[]{:S(2)}) %collective-permute-start.2) | collective-permute-done | bytes 262176 | tf_op jit(solution)/shard_map/ppermute | solution.py:33
  378.3 1.0 fusion.104
  379.3 1.9 collective-permute-start.3
  381.6 8.1 %collective-permute-done.3 = bf16[512,256]{0,1:T(8,128)(2,1)S(1)} collective-permute-done((bf16[512,256]{0,1:T(8,128)(2,1)S(1)}, bf16[512,256]{0,1:T(8,128)(2,1)S(1)}, u32[]{:S(2)}, u32[]{:S(2)}) %collective-permute-start.3) | collective-permute-done | bytes 262176 | tf_op jit(solution)/shard_map/ppermute | solution.py:33
  389.7 2.0 fusion.103
  391.7 3.6 convolution_convert_fusion.1
  395.3 38.7 %reduce-scatter.2.cloned.1.call-done = bf16[128,1024]{1,0:T(8,128)(2,1)} async-done(((bf16[1024,1024]{1,0:T(8,128)(2,1)}), bf16[128,1024]{1,0:T(8,128)(2,1)}) %reduce-scatter.2.cloned.1.call-update) | async-done | bytes 262160 | tf_op jit(solution)/shard_map/reduce_scatter | solution.py:152
  (269 shorter events, 70.8 us)
Async XLA Ops:
  6.5 320.6 %copy-start = (bf16[1024,1024]{1,0:T(8,128)(2,1)S(1)}, bf16[1024,1024]{1,0:T(8,128)(2,1)}, u32[]{:S(2)}) copy-start(bf16[1024,1024]{1,0:T(8,128)(2,1)} %param.19) | copy-start | bytes 6291460
  6.5 94.1 %all-gather.6.cloned.1.call-start = ((), (), s32[]{:S(2)}) async-start(), calls=%async_computation.1 | async-start | bytes 3727360 | tf_op jit(solution)/shard_map/all_gather | solution.py:63
  7.3 179.1 %all-gather.8.cloned.1.call-start = ((), (), s32[]{:S(2)}) async-start(), calls=%async_computation.2 | async-start | bytes 3727360 | tf_op jit(solution)/shard_map/all_gather | solution.py:70
  8.0 320.1 %all-gather.10.cloned.1.call-start = ((), (), s32[]{:S(2)}) async-start(), calls=%async_computation.4 | async-start | bytes 18874368 | tf_op jit(solution)/shard_map/all_gather | solution.py:12
  199.8 127.3 %copy-start.4 = (bf16[1024,128]{1,0:T(8,128)(2,1)S(1)}, bf16[1024,128]{1,0:T(8,128)(2,1)}, u32[]{:S(2)}) copy-start(bf16[1024,128]{1,0:T(8,128)(2,1)} %param.20) | copy-start | bytes 786436
  199.8 128.2 %copy-start.5 = (s32[1024]{0:T(1024)S(1)}, s32[1024]{0:T(1024)}, u32[]{:S(2)}) copy-start(s32[1024]{0:T(1024)} %param.23) | copy-start | bytes 12292
  199.8 234.2 %reduce-scatter.2.cloned.1.call-start = ((), (), s32[]{:S(2)}) async-start(), calls=%async_computation.3 | async-start | bytes 2359296 | tf_op jit(solution)/shard_map/reduce_scatter | solution.py:152
  338.9 3.1 copy-start.1
  338.9 3.5 copy-start.2
  344.9 10.4 %collective-permute-start = (bf16[512,256]{0,1:T(8,128)(2,1)S(1)}, bf16[512,256]{0,1:T(8,128)(2,1)S(1)}, u32[]{:S(2)}, u32[]{:S(2)}) collective-permute-start(bf16[512,256]{0,1:T(8,128)(2,1)S(1)} %bitcast.101), channel_id=1, source_target_pairs={{0,8},{8,16},{16,24},{24,32},{32,40},{40,48},{48,56},{56,64},{64,7... | collective-permute-start | bytes 786440 | tf_op jit(solution)/shard_map/ppermute | solution.py:33
  356.3 10.4 %collective-permute-start.1 = (bf16[512,256]{0,1:T(8,128)(2,1)S(1)}, bf16[512,256]{0,1:T(8,128)(2,1)S(1)}, u32[]{:S(2)}, u32[]{:S(2)}) collective-permute-start(bf16[512,256]{0,1:T(8,128)(2,1)S(1)} %collective-permute-done), channel_id=1, source_target_pairs={{0,8},{8,16},{16,24},{24,32},{32,40},{40,48},{48,56},{56,64},{64,7... | collective-permute-start | bytes 786440 | tf_op jit(solution)/shard_map/ppermute | solution.py:33
  367.7 10.5 %collective-permute-start.2 = (bf16[512,256]{0,1:T(8,128)(2,1)S(1)}, bf16[512,256]{0,1:T(8,128)(2,1)S(1)}, u32[]{:S(2)}, u32[]{:S(2)}) collective-permute-start(bf16[512,256]{0,1:T(8,128)(2,1)S(1)} %collective-permute-done.1), channel_id=1, source_target_pairs={{0,8},{8,16},{16,24},{24,32},{32,40},{40,48},{48,56},{56,64},{64,7... | collective-permute-start | bytes 786440 | tf_op jit(solution)/shard_map/ppermute | solution.py:33
  379.3 10.4 %collective-permute-start.3 = (bf16[512,256]{0,1:T(8,128)(2,1)S(1)}, bf16[512,256]{0,1:T(8,128)(2,1)S(1)}, u32[]{:S(2)}, u32[]{:S(2)}) collective-permute-start(bf16[512,256]{0,1:T(8,128)(2,1)S(1)} %collective-permute-done.2), channel_id=1, source_target_pairs={{0,8},{8,16},{16,24},{24,32},{32,40},{40,48},{48,56},{56,64},{64,7... | collective-permute-start | bytes 786440 | tf_op jit(solution)/shard_map/ppermute | solution.py:33
  389.7 2.0 copy-start.3
Sparse Core Ops, SparseCore 0:
  10.4 90.1 all-gather.5
  103.6 82.6 all-gather.7
  199.9 87.3 all-gather.9
  395.4 38.5 reduce-scatter.1
